TPU v7x, 32 devices: a whole 2x2x4 slice. The times are simulated.
32 devices in a mesh: bus: 8 (over y, x, core), period: 4 (over z).
Axes of the slice: x: 2, y: 2, z: 4, core: 2. Of those that a mesh axis runs over, the one named last changes fastest.
Arguments:
- deviation: bfloat16 [128, 256, 128], P('bus', 'period'), may hold values from -6 to 6
- loading: bfloat16 [128, 256, 128], P('bus', 'period'), may hold values from 0.5 to 2
- jacobian: bfloat16 [128, 128, 128], P('bus'), may hold values from -0.5 to 0.5
- tie_source: int32 [128, 16], P('bus'), may hold values from 0 to 127
- tie_target: int32 [128, 16], P('bus'), may hold values from 0 to 127
- tie_admittance: float32 [128, 16], P('bus'), may hold values from 0.5 to 2
- condense: bfloat16 [128, 128, 512], P('bus'), may hold values from -0.046875 to 0.046875
- section_gain: bfloat16 [4, 64, 512, 512], P('period', 'bus'), may hold values from -0.0625 to 0.0625
- retention: float32 [4, 64, 512], P('period', 'bus'), may hold values from 0 to 1
Outputs:
- mismatch: bfloat16 [128, 256, 128], P('bus', 'period')
- section_states: float32 [4, 64, 512], P('period', 'bus')
All inputs are finite; a program needn't handle non-finite values.
Results may differ from a plain program's by a relative error of at most 0.013.
Values may be sent and summed in bfloat16 or wider, within the bound.
No kernel may reach another device: no remote copies, remote signals or barrier semaphores. Data moves between devices by JAX's collectives and lax.ppermute only.
A program may use at most 64 MiB of HBM per device.

v0:
```python
import jax
import jax.numpy as jnp
from jax import lax
from jax.sharding import PartitionSpec as P


def from_behind(value, axis, steps):
    count = lax.axis_size(axis)
    leading, last = (max(0, -steps), min(count, count - steps))
    return lax.ppermute(value, axis, [(source, source + steps) for source in range(leading, last)])


def entering_2(value, axis, combine, identity):
    size, place = (lax.axis_size(axis), lax.axis_index(axis))
    everything = jax.tree.map(lambda part: lax.all_gather(part, axis), value)
    start = jax.tree.map(
        lambda part, zero: jnp.broadcast_to(jnp.asarray(zero, part.dtype), part.shape),
        value,
        identity,
    )

    def step(k, before):
        reached = k < place
        new = combine(before, jax.tree.map(lambda part: part[k], everything))
        return jax.tree.map(lambda a, b: jnp.where(reached, a, b), new, before)

    return lax.fori_loop(0, size, step, start)


def broadcast(block, axis, owner):
    block = jnp.where(lax.axis_index(axis) == owner, block, jnp.zeros_like(block))
    return lax.psum(block, axis)


def combine(earlier, later):
    return (earlier[0] * later[0], later[0] * earlier[1] + later[1])


def place(flows, hot):
    upper = flows.astype(jnp.bfloat16)
    lower = (flows - upper.astype(jnp.float32)).astype(jnp.bfloat16)
    both = jnp.concatenate([upper, lower], axis=2)
    hot_twice = jnp.concatenate([hot, hot], axis=1)
    return jnp.einsum("bte,beq->btq", both, hot_twice, preferred_element_type=jnp.float32)


def shards(
    deviation,
    loading,
    jacobian,
    tie_source,
    tie_target,
    tie_admittance,
    condense,
    section_gain,
    retention,
):
    block_width = deviation.shape[2]
    scaled = (deviation.astype(jnp.float32) * loading.astype(jnp.float32)).astype(jnp.bfloat16)
    columns = jnp.arange(block_width, dtype=jnp.int32)
    source_hot = (tie_source[:, :, None] == columns[None, None, :]).astype(jnp.bfloat16)
    target_hot = (tie_target[:, :, None] == columns[None, None, :]).astype(jnp.bfloat16)
    next_first = from_behind(scaled[0], "bus", -1)
    next_block = jnp.concatenate([scaled[1:], next_first[None]], axis=0)
    at_target = jnp.einsum(
        "btq,beq->bte", next_block, target_hot, preferred_element_type=jnp.float32
    )
    network = jnp.einsum("btp,bpq->btq", scaled, jacobian, preferred_element_type=jnp.float32)
    at_source = jnp.einsum("btq,beq->bte", scaled, source_hot, preferred_element_type=jnp.float32)
    edge_flow = tie_admittance[:, None, :] * (at_target - at_source)
    own_terms = place(edge_flow, source_hot)
    handed = -place(edge_flow, target_hot)
    incoming = from_behind(handed[-1], "bus", 1)
    received = jnp.concatenate([incoming[None], handed[:-1]], axis=0)
    mismatch = (network + own_terms + received).astype(jnp.bfloat16)
    span_rows = section_gain.shape[1]
    partial_value = jnp.einsum(
        "btq,bqm->tm", mismatch, condense, preferred_element_type=jnp.float32
    )
    totals = lax.psum(partial_value, "bus")
    section_sum = lax.dynamic_slice_in_dim(totals, lax.axis_index("bus") * span_rows, span_rows, 0)
    section_in = section_sum.astype(jnp.bfloat16)
    pushed = jnp.einsum(
        "tm,tmn->tn", section_in, section_gain[0], preferred_element_type=jnp.float32
    )
    states_width = pushed.shape[1]
    ones_row = jnp.ones((states_width,), jnp.float32)
    zeros_row = jnp.zeros((states_width,), jnp.float32)

    def advance(carried, inputs):
        section_now, product = carried
        retain, pushed_now = inputs
        section_now = retain * section_now + pushed_now
        product = product * retain
        return ((section_now, product), (section_now, product))

    (last_state, span_rate), (local_states, running) = lax.scan(
        advance, (zeros_row, ones_row), (retention[0], pushed)
    )
    own_map = (span_rate, last_state)
    identity = (ones_row, zeros_row)
    before = entering_2(own_map, "bus", combine, identity)
    through = combine(before, own_map)
    group_map = (
        broadcast(through[0], "bus", lax.axis_size("bus") - 1),
        broadcast(through[1], "bus", lax.axis_size("bus") - 1),
    )
    across = entering_2(group_map, "period", combine, identity)
    entering = combine(across, before)[1]
    states = local_states + running * entering[None, :]
    return (mismatch, states[None])


def solution(mesh):
    placed = (
        P("bus", "period", None),
        P("bus", "period", None),
        P("bus", None, None),
        P("bus", None),
        P("bus", None),
        P("bus", None),
        P("bus", None, None),
        P("period", "bus", None, None),
        P("period", "bus", None),
    )
    return jax.shard_map(
        shards,
        mesh=mesh,
        in_specs=placed,
        out_specs=(P("bus", "period", None), P("period", "bus", None)),
        check_vma=False,
    )
```

profile of v0, /device:TPU:0, one launch (start us, length us, event | category | flops | bytes accessed | tf_op | source)
XLA Modules:
  0.0 106.2 jit_solution(14670595446566683150)
XLA Ops:
  0.7 1.3 %multiply_convert_fusion = bf16[16,64,128]{2,1,0:T(8,128)(2,1)S(1)} fusion(bf16[16,64,128]{2,1,0:T(8,128)(2,1)} %param.16, bf16[16,64,128]{2,1,0:T(8,128)(2,1)} %param.15), kind=kLoop, calls=%fused_computation.21 | loop fusion | flops 524288 | bytes 786432 | tf_op jit(solution)/shard_map/convert_element_type | solution.py:59
  1.9 1.3 %collective-permute-start = (bf16[64,128]{1,0:T(8,128)(2,1)S(1)}, bf16[64,128]{1,0:T(8,128)(2,1)S(1)}, u32[]{:S(2)}, u32[]{:S(2)}) collective-permute-start(bf16[64,128]{1,0:T(8,128)(2,1)S(1)} %slice_bitcast_fusion.1), channel_id=1, source_target_pairs={{4,0},{8,4},{12,8},{16,12},{20,16},{24,20},{28,24},{5,1},{9,5},{13... | collective-permute-start | bytes 49160 | tf_op jit(solution)/shard_map/ppermute | solution.py:10
  3.2 1.0 fusion.23
  4.2 1.3 %fusion.25 = f32[16,64,128]{2,1,0:T(8,128)S(1)} fusion(bf16[16,64,128]{2,1,0:T(8,128)(2,1)S(1)} %multiply_convert_fusion, bf16[16,128,128]{2,1,0:T(8,128)(2,1)} %param.17), kind=kOutput, calls=%fused_computation.56 | convolution fusion | flops 33554432 | bytes 1310720 | tf_op jit(solution)/shard_map/btp,bpq->btq/dot_general | solution.py:68
  5.5 0.8 iota_compare_fusion.1
  6.4 1.0 fusion.24
  7.7 3.8 %collective-permute-start.1 = (f32[64,128]{1,0:T(8,128)S(1)}, f32[64,128]{1,0:T(8,128)S(1)}, u32[]{:S(2)}, u32[]{:S(2)}) collective-permute-start(f32[64,128]{1,0:T(8,128)S(1)} %slice_bitcast_fusion), channel_id=1, source_target_pairs={{0,4},{4,8},{8,12},{12,16},{16,20},{20,24},{24,28},{1,5},{5,9},{9,... | collective-permute-start | bytes 98312 | tf_op jit(solution)/shard_map/ppermute | solution.py:10
  13.2 26.5 %all-reduce.2 = bf16[64,512]{1,0:T(8,128)(2,1)S(1)} all-reduce(f32[64,512]{1,0:T(8,128)S(1)} %convolution_bitcast_fusion), channel_id=1, replica_groups=mesh['bus'=8,'period'=4] {'bus'}, use_global_device_ids=true, to_apply=%region_0.0 | all-reduce | flops 32768 | bytes 196608 | tf_op jit(solution)/shard_map/psum | solution.py:80
  39.7 2.8 %fusion.1 = f32[8,1,512]{2,1,0:T(1,128)S(1)} fusion(bf16[1,8,512,512]{3,2,1,0:T(8,128)(2,1)} %param.22, bf16[8,512,1]{1,0,2:T(8,128)(2,1)S(1)} %fusion.17), kind=kOutput, calls=%fused_computation.12 | convolution fusion | flops 4194304 | bytes 4218880 | tf_op jit(solution)/shard_map/tm,tmn->tn/dot_general | solution.py:83
  42.5 7.1 %while.47 = (s32[]{:T(128)}, f32[512]{0:T(512)S(1)}, f32[512]{0:T(512)S(1)}, f32[8,512]{1,0:T(8,128)S(1)}, f32[8,512]{1,0:T(8,128)S(1)}, /*index=5*/f32[8,512]{1...) while((s32[]{:T(128)}, f32[512]{0:T(512)S(1)}, f32[512]{0:T(512)S(1)}, f32[8,512]{1,0:T(8,128)S(1)}, ...), condition=%wide.region_2.3_spmd.clone, body=%wide.region_1.2_spmd.clone.sunk | while | flops 2563 | bytes 28787 | solution.py:97
  42.5 0.7 constant_dynamic-slice_fusion.9
  43.4 0.7 constant_dynamic-slice_fusion.9
  44.3 0.7 constant_dynamic-slice_fusion.9
  45.2 0.7 constant_dynamic-slice_fusion.9
  46.1 0.7 constant_dynamic-slice_fusion.9
  47.0 0.7 constant_dynamic-slice_fusion.9
  47.9 0.7 constant_dynamic-slice_fusion.9
  48.8 0.7 constant_dynamic-slice_fusion.9
  49.7 10.4 %all-gather.3 = f32[8,1,512]{2,1,0:T(1,128)S(1)} all-gather(f32[1,1,512]{2,1,0:T(1,128)S(1)} %bitcast.67), channel_id=3, replica_groups=mesh['bus'=8,'period'=4] {'bus'}, dimensions={0}, use_global_device_ids=true | all-gather | bytes 18432 | tf_op jit(solution)/shard_map/all_gather | solution.py:15
  60.0 7.7 %all-gather.2 = f32[8,1,512]{2,1,0:T(1,128)S(1)} all-gather(f32[1,1,512]{2,1,0:T(1,128)S(1)} %bitcast.69), channel_id=2, replica_groups=mesh['bus'=8,'period'=4] {'bus'}, dimensions={0}, use_global_device_ids=true | all-gather | bytes 18432 | tf_op jit(solution)/shard_map/all_gather | solution.py:15
  68.2 13.2 %all-reduce = (f32[1,512]{1,0:T(1,128)S(1)}, f32[1,512]{1,0:T(1,128)S(1)}) all-reduce(f32[1,512]{1,0:T(1,128)S(1)} %bitcast.83, f32[1,512]{1,0:T(1,128)S(1)} %bitcast.82), channel_id=1, replica_groups=mesh['bus'=8,'period'=4] {'bus'}, use_global_device_ids=true, to_apply=%region_5.6 | all-reduce | flops 1024 | bytes 8192 | tf_op jit(solution)/shard_map/psum | solution.py:32
  81.4 12.1 %all-gather.5 = f32[4,1,512]{2,1,0:T(1,128)S(1)} all-gather(f32[1,1,512]{2,1,0:T(1,128)S(1)} %bitcast.86), channel_id=1, replica_groups=mesh['bus'=8,'period'=4] {'period'}, dimensions={0}, use_global_device_ids=true | all-gather | bytes 10240 | tf_op jit(solution)/shard_map/all_gather | solution.py:15
  93.5 11.9 %all-gather.4 = f32[4,1,512]{2,1,0:T(1,128)S(1)} all-gather(f32[1,1,512]{2,1,0:T(1,128)S(1)} %bitcast.85), channel_id=1, replica_groups=mesh['bus'=8,'period'=4] {'period'}, dimensions={0}, use_global_device_ids=true | all-gather | bytes 10240 | tf_op jit(solution)/shard_map/all_gather | solution.py:15
  105.6 0.6 add_bitcast_fusion
  (81 shorter events, 3.8 us)
Async XLA Ops:
  0.6 12.0 %copy-start = (bf16[16,128,512]{2,1,0:T(8,128)(2,1)S(1)}, bf16[16,128,512]{2,1,0:T(8,128)(2,1)}, u32[]{:S(2)}) copy-start(bf16[16,128,512]{2,1,0:T(8,128)(2,1)} %param.21) | copy-start | bytes 6291460
  0.6 10.9 %copy-start.2 = (s32[16,16]{1,0:T(8,128)S(1)}, s32[16,16]{1,0:T(8,128)}, u32[]{:S(2)}) copy-start(s32[16,16]{1,0:T(8,128)} %param.18) | copy-start | bytes 3076
  1.9 4.5 %collective-permute-start = (bf16[64,128]{1,0:T(8,128)(2,1)S(1)}, bf16[64,128]{1,0:T(8,128)(2,1)S(1)}, u32[]{:S(2)}, u32[]{:S(2)}) collective-permute-start(bf16[64,128]{1,0:T(8,128)(2,1)S(1)} %slice_bitcast_fusion.1), channel_id=1, source_target_pairs={{4,0},{8,4},{12,8},{16,12},{20,16},{24,20},{28,24},{5,1},{9,5},{13... | collective-permute-start | bytes 49160 | tf_op jit(solution)/shard_map/ppermute | solution.py:10
  7.7 4.7 %collective-permute-start.1 = (f32[64,128]{1,0:T(8,128)S(1)}, f32[64,128]{1,0:T(8,128)S(1)}, u32[]{:S(2)}, u32[]{:S(2)}) collective-permute-start(f32[64,128]{1,0:T(8,128)S(1)} %slice_bitcast_fusion), channel_id=1, source_target_pairs={{0,4},{4,8},{8,12},{12,16},{16,20},{20,24},{24,28},{1,5},{5,9},{9,... | collective-permute-start | bytes 98312 | tf_op jit(solution)/shard_map/ppermute | solution.py:10
  12.7 93.5 %copy-start.1 = (bf16[16,64,128]{2,1,0:T(8,128)(2,1)}, bf16[16,64,128]{2,1,0:T(8,128)(2,1)S(1)}, u32[]{:S(2)}) copy-start(bf16[16,64,128]{2,1,0:T(8,128)(2,1)S(1)} %fusion.4) | copy-start | bytes 786436
where the time goes:
time: 107 us; the launch traced here: 106 us
  blocking collectives  81.7 us (76%)
  matrix products  7.18 us (7%)
  local copies, waits for them, and re-layouts  7.02 us (7%)
  starting transfers between devices  5.11 us (5%)
  other arithmetic  3.07 us (3%)
    all_gather x4, blocking collectives, entering_2(): everything = jax.tree.map(lambda part: lax.all_gather(part, axis), value)  42 us
    psum x1, blocking collectives, shards(): totals = lax.psum(partial_value, 'bus')  26.5 us
    psum x1, blocking collectives, broadcast(): return lax.psum(block, axis)  13.2 us
    dynamic_slice x8, local copies, waits for them, and re-layouts, shards(): lax.scan(advance, (zeros_row, ones_row), (retention[0], pushed))  5.84 us
    ppermute x2, starting transfers between devices, from_behind(): lax.ppermute(value, axis, [(source, source + steps) for source in range(l...  5.11 us
    dot_general x1, matrix products, shards(): jnp.einsum('tm,tmn->tn', section_in, section_gain[0], preferred_element_t...  2.83 us
  transfers between devices with their start and end apart: 2, of which 1 were waited for; matrix products, arithmetic and copies ran while one was open for 3% of the time, Pallas kernels for 0%

commit v1 on v0

--- a/solution.py
+++ b/solution.py
@@ -77,7 +77,9 @@
     partial_value = jnp.einsum(
         "btq,bqm->tm", mismatch, condense, preferred_element_type=jnp.float32
     )
-    totals = lax.psum(partial_value, "bus")
+    totals = partial_value
+    for hop in (1, 2, 4):
+        totals = totals + lax.ppermute(totals, "bus", [(dev, dev ^ hop) for dev in range(8)])
     section_sum = lax.dynamic_slice_in_dim(totals, lax.axis_index("bus") * span_rows, span_rows, 0)
     section_in = section_sum.astype(jnp.bfloat16)
     pushed = jnp.einsum(

time: 107 us -> 96 us (0.90)
  blocking collectives: 81.7 us -> 54.3 us
  starting transfers between devices: 5.11 us -> 13.3 us
  waiting for transfers between devices: 0.6 us -> 8.45 us
    psum x1 -> x0, blocking collectives: 26.5 us -> none  [shards(): totals = lax.psum(partial_value, 'bus')]
    ppermute x0 -> x3, starting transfers between devices: none -> 8.22 us  [shards(): lax.ppermute(totals, 'bus', [(dev, dev ^ hop) for dev in range(8)])]
    ppermute x0 -> x3, waiting for transfers between devices: none -> 7.77 us  [shards(): lax.ppermute(totals, 'bus', [(dev, dev ^ hop) for dev in range(8)])]
  transfers between devices with their start and end apart: 2 -> 5, of which waited for: 1 -> 4; matrix products, arithmetic and copies ran while one was open for 3% -> 3% of each run, Pallas kernels for 0% -> 0%
where the time goes in v1:
time: 96 us; the launch traced here: 94.8 us
  blocking collectives  54.3 us (57%)
  starting transfers between devices  13.3 us (14%)
  waiting for transfers between devices  8.45 us (9%)
  matrix products  7.18 us (7%)
  local copies, waits for them, and re-layouts  7 us (7%)
  other arithmetic  3.11 us (3%)
    all_gather x4, blocking collectives, entering_2(): everything = jax.tree.map(lambda part: lax.all_gather(part, axis), value)  41.1 us
    psum x1, blocking collectives, broadcast(): return lax.psum(block, axis)  13.2 us
    ppermute x3, starting transfers between devices, shards(): lax.ppermute(totals, 'bus', [(dev, dev ^ hop) for dev in range(8)])  8.22 us
    ppermute x3, waiting for transfers between devices, shards(): lax.ppermute(totals, 'bus', [(dev, dev ^ hop) for dev in range(8)])  7.77 us
    dynamic_slice x8, local copies, waits for them, and re-layouts, shards(): lax.scan(advance, (zeros_row, ones_row), (retention[0], pushed))  5.84 us
    ppermute x2, starting transfers between devices, from_behind(): lax.ppermute(value, axis, [(source, source + steps) for source in range(l...  5.11 us
    dot_general x1, matrix products, shards(): jnp.einsum('tm,tmn->tn', section_in, section_gain[0], preferred_element_t...  2.83 us
  transfers between devices with their start and end apart: 5, of which 4 were waited for; matrix products, arithmetic and copies ran while one was open for 3% of the time, Pallas kernels for 0%

profile of v1, /device:TPU:0, one launch (start us, length us, event | category | flops | bytes accessed | tf_op | source)
XLA Modules:
  0.0 94.8 jit_solution(2007202666782782830)
XLA Ops:
  0.7 1.3 %multiply_convert_fusion = bf16[16,64,128]{2,1,0:T(8,128)(2,1)S(1)} fusion(bf16[16,64,128]{2,1,0:T(8,128)(2,1)} %param.16, bf16[16,64,128]{2,1,0:T(8,128)(2,1)} %param.15), kind=kLoop, calls=%fused_computation.21 | loop fusion | flops 524288 | bytes 786432 | tf_op jit(solution)/shard_map/convert_element_type | solution.py:59
  1.9 1.3 %collective-permute-start = (bf16[64,128]{1,0:T(8,128)(2,1)S(1)}, bf16[64,128]{1,0:T(8,128)(2,1)S(1)}, u32[]{:S(2)}, u32[]{:S(2)}) collective-permute-start(bf16[64,128]{1,0:T(8,128)(2,1)S(1)} %slice_bitcast_fusion.1), channel_id=1, source_target_pairs={{4,0},{8,4},{12,8},{16,12},{20,16},{24,20},{28,24},{5,1},{9,5},{13... | collective-permute-start | bytes 49160 | tf_op jit(solution)/shard_map/ppermute | solution.py:10
  3.2 1.0 %fusion.24 = f32[16,64,16]{1,2,0:T(8,128)S(1)} fusion(bf16[16,64,128]{2,1,0:T(8,128)(2,1)S(1)} %multiply_convert_fusion, s32[16,16]{1,0:T(8,128)} %param.18), kind=kOutput, calls=%fused_computation.55 | convolution fusion | flops 4227072 | bytes 328704 | tf_op jit(solution)/shard_map/btq,beq->bte/dot_general | solution.py:69
  4.2 1.3 %fusion.26 = f32[16,64,128]{2,1,0:T(8,128)S(1)} fusion(bf16[16,64,128]{2,1,0:T(8,128)(2,1)S(1)} %multiply_convert_fusion, bf16[16,128,128]{2,1,0:T(8,128)(2,1)} %param.17), kind=kOutput, calls=%fused_computation.57 | convolution fusion | flops 33554432 | bytes 1310720 | tf_op jit(solution)/shard_map/btp,bpq->btq/dot_general | solution.py:68
  5.5 0.8 iota_compare_fusion.1
  6.4 1.0 %fusion.25 = (bf16[16,64,16]{1,2,0:T(8,128)(2,1)S(1)}, bf16[16,64,16]{1,2,0:T(8,128)(2,1)S(1)}) fusion(f32[16,64,16]{1,2,0:T(8,128)S(1)} %fusion.24, s32[16,16]{1,0:T(8,128)} %param.19, bf16[1,64,128]{2,1,0:T(8,128)(2,1)S(1)} %bitcast.87, bf16[15,64,128]{2,1,0:T(8,128)(2,1)S(1)} %slice.16, f32[16,16]{1,0:T(8,128)} %param.20), kind=kOutput, calls=%fused_computation.56 | convolution fusion | flops 4456448 | bytes 395264 | tf_op jit(solution)/shard_map/btq,beq->bte/dot_general | solution.py:65
  7.7 3.8 %collective-permute-start.1 = (f32[64,128]{1,0:T(8,128)S(1)}, f32[64,128]{1,0:T(8,128)S(1)}, u32[]{:S(2)}, u32[]{:S(2)}) collective-permute-start(f32[64,128]{1,0:T(8,128)S(1)} %slice_bitcast_fusion), channel_id=1, source_target_pairs={{0,4},{4,8},{8,12},{12,16},{16,20},{20,24},{24,28},{1,5},{5,9},{9,... | collective-permute-start | bytes 98312 | tf_op jit(solution)/shard_map/ppermute | solution.py:10
  13.2 2.0 %collective-permute-start.2 = (f32[64,512]{1,0:T(8,128)S(1)}, f32[64,512]{1,0:T(8,128)S(1)}, u32[]{:S(2)}, u32[]{:S(2)}) collective-permute-start(f32[64,512]{1,0:T(8,128)S(1)} %convolution_bitcast_fusion), channel_id=1, source_target_pairs={{0,4},{4,0},{8,12},{12,8},{16,20},{20,16},{24,28},{28,24},{1,5},{5... | collective-permute-start | bytes 393224 | tf_op jit(solution)/shard_map/ppermute | solution.py:82
  15.2 1.0 %collective-permute-done.2 = f32[64,512]{1,0:T(8,128)S(1)} collective-permute-done((f32[64,512]{1,0:T(8,128)S(1)}, f32[64,512]{1,0:T(8,128)S(1)}, u32[]{:S(2)}, u32[]{:S(2)}) %collective-permute-start.2) | collective-permute-done | bytes 131104 | tf_op jit(solution)/shard_map/ppermute | solution.py:82
  16.2 2.6 %collective-permute-start.3 = (f32[64,512]{1,0:T(8,128)S(1)}, f32[64,512]{1,0:T(8,128)S(1)}, u32[]{:S(2)}, u32[]{:S(2)}) collective-permute-start(f32[64,512]{1,0:T(8,128)S(1)} %add.97), channel_id=1, source_target_pairs={{0,8},{4,12},{8,0},{12,4},{16,24},{20,28},{24,16},{28,20},{1,9},{5... | collective-permute-start | bytes 393224 | tf_op jit(solution)/shard_map/ppermute | solution.py:82
  18.8 3.8 %collective-permute-done.3 = f32[64,512]{1,0:T(8,128)S(1)} collective-permute-done((f32[64,512]{1,0:T(8,128)S(1)}, f32[64,512]{1,0:T(8,128)S(1)}, u32[]{:S(2)}, u32[]{:S(2)}) %collective-permute-start.3) | collective-permute-done | bytes 131104 | tf_op jit(solution)/shard_map/ppermute | solution.py:82
  22.6 3.6 %collective-permute-start.4 = (f32[64,512]{1,0:T(8,128)S(1)}, f32[64,512]{1,0:T(8,128)S(1)}, u32[]{:S(2)}, u32[]{:S(2)}) collective-permute-start(f32[64,512]{1,0:T(8,128)S(1)} %add.98), channel_id=1, source_target_pairs={{0,16},{4,20},{8,24},{12,28},{16,0},{20,4},{24,8},{28,12},{1,17},{... | collective-permute-start | bytes 393224 | tf_op jit(solution)/shard_map/ppermute | solution.py:82
  26.2 3.0 %collective-permute-done.4 = f32[64,512]{1,0:T(8,128)S(1)} collective-permute-done((f32[64,512]{1,0:T(8,128)S(1)}, f32[64,512]{1,0:T(8,128)S(1)}, u32[]{:S(2)}, u32[]{:S(2)}) %collective-permute-start.4) | collective-permute-done | bytes 131104 | tf_op jit(solution)/shard_map/ppermute | solution.py:82
  29.2 2.8 %fusion.1 = f32[8,1,512]{2,1,0:T(1,128)S(1)} fusion(bf16[1,8,512,512]{3,2,1,0:T(8,128)(2,1)} %param.22, bf16[8,512,1]{1,0,2:T(8,128)(2,1)S(1)} %fusion.18), kind=kOutput, calls=%fused_computation.12 | convolution fusion | flops 4194304 | bytes 4218880 | tf_op jit(solution)/shard_map/tm,tmn->tn/dot_general | solution.py:85
  32.0 7.1 %while.47 = (s32[]{:T(128)}, f32[512]{0:T(512)S(1)}, f32[512]{0:T(512)S(1)}, f32[8,512]{1,0:T(8,128)S(1)}, f32[8,512]{1,0:T(8,128)S(1)}, /*index=5*/f32[8,512]{1...) while((s32[]{:T(128)}, f32[512]{0:T(512)S(1)}, f32[512]{0:T(512)S(1)}, f32[8,512]{1,0:T(8,128)S(1)}, ...), condition=%wide.region_1.2_spmd.clone, body=%wide.region_0.1_spmd.clone.sunk | while | flops 2563 | bytes 28787 | solution.py:99
  32.0 0.7 constant_dynamic-slice_fusion.9
  34.7 0.7 constant_dynamic-slice_fusion.9
  35.6 0.7 constant_dynamic-slice_fusion.9
  36.5 0.7 constant_dynamic-slice_fusion.9
  39.2 9.4 %all-gather.3 = f32[8,1,512]{2,1,0:T(1,128)S(1)} all-gather(f32[1,1,512]{2,1,0:T(1,128)S(1)} %bitcast.67), channel_id=3, replica_groups=mesh['bus'=8,'period'=4] {'bus'}, dimensions={0}, use_global_device_ids=true | all-gather | bytes 18432 | tf_op jit(solution)/shard_map/all_gather | solution.py:15
  48.6 7.7 %all-gather.2 = f32[8,1,512]{2,1,0:T(1,128)S(1)} all-gather(f32[1,1,512]{2,1,0:T(1,128)S(1)} %bitcast.69), channel_id=2, replica_groups=mesh['bus'=8,'period'=4] {'bus'}, dimensions={0}, use_global_device_ids=true | all-gather | bytes 18432 | tf_op jit(solution)/shard_map/all_gather | solution.py:15
  56.8 13.2 %all-reduce = (f32[1,512]{1,0:T(1,128)S(1)}, f32[1,512]{1,0:T(1,128)S(1)}) all-reduce(f32[1,512]{1,0:T(1,128)S(1)} %bitcast.83, f32[1,512]{1,0:T(1,128)S(1)} %bitcast.82), channel_id=1, replica_groups=mesh['bus'=8,'period'=4] {'bus'}, use_global_device_ids=true, to_apply=%region_4.5 | all-reduce | flops 1024 | bytes 8192 | tf_op jit(solution)/shard_map/psum | solution.py:32
  70.0 12.1 %all-gather.5 = f32[4,1,512]{2,1,0:T(1,128)S(1)} all-gather(f32[1,1,512]{2,1,0:T(1,128)S(1)} %bitcast.86), channel_id=1, replica_groups=mesh['bus'=8,'period'=4] {'period'}, dimensions={0}, use_global_device_ids=true | all-gather | bytes 10240 | tf_op jit(solution)/shard_map/all_gather | solution.py:15
  82.1 11.9 %all-gather.4 = f32[4,1,512]{2,1,0:T(1,128)S(1)} all-gather(f32[1,1,512]{2,1,0:T(1,128)S(1)} %bitcast.85), channel_id=1, replica_groups=mesh['bus'=8,'period'=4] {'period'}, dimensions={0}, use_global_device_ids=true | all-gather | bytes 10240 | tf_op jit(solution)/shard_map/all_gather | solution.py:15
  (88 shorter events, 7.5 us)
Async XLA Ops:
  0.6 12.0 %copy-start = (bf16[16,128,512]{2,1,0:T(8,128)(2,1)S(1)}, bf16[16,128,512]{2,1,0:T(8,128)(2,1)}, u32[]{:S(2)}) copy-start(bf16[16,128,512]{2,1,0:T(8,128)(2,1)} %param.21) | copy-start | bytes 6291460
  0.6 10.9 %copy-start.2 = (s32[16,16]{1,0:T(8,128)S(1)}, s32[16,16]{1,0:T(8,128)}, u32[]{:S(2)}) copy-start(s32[16,16]{1,0:T(8,128)} %param.18) | copy-start | bytes 3076
  1.9 4.5 %collective-permute-start = (bf16[64,128]{1,0:T(8,128)(2,1)S(1)}, bf16[64,128]{1,0:T(8,128)(2,1)S(1)}, u32[]{:S(2)}, u32[]{:S(2)}) collective-permute-start(bf16[64,128]{1,0:T(8,128)(2,1)S(1)} %slice_bitcast_fusion.1), channel_id=1, source_target_pairs={{4,0},{8,4},{12,8},{16,12},{20,16},{24,20},{28,24},{5,1},{9,5},{13... | collective-permute-start | bytes 49160 | tf_op jit(solution)/shard_map/ppermute | solution.py:10
  7.7 4.7 %collective-permute-start.1 = (f32[64,128]{1,0:T(8,128)S(1)}, f32[64,128]{1,0:T(8,128)S(1)}, u32[]{:S(2)}, u32[]{:S(2)}) collective-permute-start(f32[64,128]{1,0:T(8,128)S(1)} %slice_bitcast_fusion), channel_id=1, source_target_pairs={{0,4},{4,8},{8,12},{12,16},{16,20},{20,24},{24,28},{1,5},{5,9},{9,... | collective-permute-start | bytes 98312 | tf_op jit(solution)/shard_map/ppermute | solution.py:10
  12.7 43.6 %copy-start.1 = (bf16[16,64,128]{2,1,0:T(8,128)(2,1)}, bf16[16,64,128]{2,1,0:T(8,128)(2,1)S(1)}, u32[]{:S(2)}) copy-start(bf16[16,64,128]{2,1,0:T(8,128)(2,1)S(1)} %fusion.4) | copy-start | bytes 786436
  13.2 3.0 %collective-permute-start.2 = (f32[64,512]{1,0:T(8,128)S(1)}, f32[64,512]{1,0:T(8,128)S(1)}, u32[]{:S(2)}, u32[]{:S(2)}) collective-permute-start(f32[64,512]{1,0:T(8,128)S(1)} %convolution_bitcast_fusion), channel_id=1, source_target_pairs={{0,4},{4,0},{8,12},{12,8},{16,20},{20,16},{24,28},{28,24},{1,5},{5... | collective-permute-start | bytes 393224 | tf_op jit(solution)/shard_map/ppermute | solution.py:82
  16.2 6.4 %collective-permute-start.3 = (f32[64,512]{1,0:T(8,128)S(1)}, f32[64,512]{1,0:T(8,128)S(1)}, u32[]{:S(2)}, u32[]{:S(2)}) collective-permute-start(f32[64,512]{1,0:T(8,128)S(1)} %add.97), channel_id=1, source_target_pairs={{0,8},{4,12},{8,0},{12,4},{16,24},{20,28},{24,16},{28,20},{1,9},{5... | collective-permute-start | bytes 393224 | tf_op jit(solution)/shard_map/ppermute | solution.py:82
  22.6 6.6 %collective-permute-start.4 = (f32[64,512]{1,0:T(8,128)S(1)}, f32[64,512]{1,0:T(8,128)S(1)}, u32[]{:S(2)}, u32[]{:S(2)}) collective-permute-start(f32[64,512]{1,0:T(8,128)S(1)} %add.98), channel_id=1, source_target_pairs={{0,16},{4,20},{8,24},{12,28},{16,0},{20,4},{24,8},{28,12},{1,17},{... | collective-permute-start | bytes 393224 | tf_op jit(solution)/shard_map/ppermute | solution.py:82
